TPU v7x, 32 devices: a whole 2x2x4 slice. The times are simulated.
32 devices in a mesh: group: 8 (over z, x), owner: 4 (over y, core).
Axes of the slice: x: 2, y: 2, z: 4, core: 2. Of those that a mesh axis runs over, the one named last changes fastest.
Arguments:
- embeddings: bfloat16 [32768, 1024], P(('group', 'owner')), may hold values from -2 to 2
- home_pairs: int32 [8, 4, 3, 64, 2], P('group', 'owner'), may hold values from 0 to 7, as said below
- home_count: int32 [8, 4, 3], P('group', 'owner'), may hold values from 0 to 28
- surplus_pairs: int32 [8, 4, 8, 3], P('group', 'owner'), may hold values from 0 to 7, as said below
Outputs:
- centered: bfloat16 [32768, 1024], P(('group', 'owner'))
- log_density: float32 [32768], P(('group', 'owner'))
Inputs may be any that keep to these rules, and one draw needn't show every extreme that they name: `home_pairs`: for owner o of group g and distance s, the first home_count[g, o, s] slots hold distinct pairs (a, b) of block a of owner o and block b of owner (o + s) mod 4 that lie in one cluster; at distance 0 a <= b and every pair (a, a) is listed; at twice s equal to 4 only owners below 2 list pairs; later slots are ignored. `surplus_pairs`: A live entry (a, b, 1) names two blocks of the same owner in one cluster with a < b; no pair is live twice or also listed in home_pairs; dead entries are ignored.
All inputs are finite; a program needn't handle non-finite values.
Results may differ from a plain program's by a relative error of at most 0.0057.
Values may be sent and summed in bfloat16 or wider, within the bound.
A program may use at most 128 MiB of HBM per device.

v0:
```python
import functools

import jax
import jax.numpy as jnp
from jax import lax
from jax.experimental import pallas as pl
from jax.experimental.pallas import tpu as pltpu
from jax.sharding import PartitionSpec as P

BLOCK = 128
LANES = 128
VMEM_BYTES = 56 * 1024 * 1024

sharpness = 4.0
epsilon = 1e-06

VMEM = pltpu.MemorySpace.VMEM
SMEM = pltpu.MemorySpace.SMEM
ANY = pl.ANY


def kernel_of(first, second):
    width = first.shape[-1]
    similarity = lax.dot_general(
        first, second, (((1,), (1,)), ((), ())), preferred_element_type=jnp.float32
    ) * (1.0 / width)
    return jnp.exp(sharpness * (similarity - 1.0))


def prep_kernel(shifts, surplus, lists_ref, emb_ref, unit_ref, mask_ref):
    blocks = unit_ref.shape[0]
    mask_ref[...] = jnp.zeros_like(mask_ref)
    one = jnp.ones((1, BLOCK), jnp.float32)

    def mark(a, b):
        mask_ref[a, :, pl.ds(pl.multiple_of(b * BLOCK, BLOCK), BLOCK)] = one
        mask_ref[b, :, pl.ds(pl.multiple_of(a * BLOCK, BLOCK), BLOCK)] = one

    @pl.loop(0, lists_ref[shifts, 0])
    def _(t):
        mark(lists_ref[0, 2 * t], lists_ref[0, 2 * t + 1])

    @pl.loop(0, surplus)
    def _(t):
        @pl.when(lists_ref[2 * shifts, 3 * t + 2] == 1)
        def _():
            mark(lists_ref[2 * shifts, 3 * t], lists_ref[2 * shifts, 3 * t + 1])

    @pl.loop(0, blocks)
    def _(i):
        wide = emb_ref[i].astype(jnp.float32)
        inv = lax.rsqrt(jnp.mean(wide * wide, axis=-1, keepdims=True) + epsilon)
        unit_ref[i] = (wide * inv).astype(jnp.bfloat16)


def exchange_kernel(
    n, unit_ref, lists_ref, mask_ref, recv_ref, all_lists_ref, acc_ref, dens_ref,
    send_sem, recv_sem, side_send, side_recv, fwd_send, fwd_recv, list_send, list_recv,
):
    me = lax.axis_index("owner")
    blocks = unit_ref.shape[0]
    width = unit_ref.shape[2]
    chips = n // 2
    sibling = me + 1 - 2 * lax.rem(me, 2)

    barrier = pltpu.get_barrier_semaphore()
    for d in range(1, n):
        pl.semaphore_signal(barrier, inc=1, device_id={"owner": lax.rem(me + d, n)})
    pl.semaphore_wait(barrier, n - 1)

    def list_copy(d):
        return pltpu.make_async_remote_copy(
            src_ref=lists_ref, dst_ref=all_lists_ref.at[me],
            send_sem=list_send.at[d], recv_sem=list_recv.at[d],
            device_id={"owner": lax.rem(me + d, n)},
        )

    def cross_copy(k, i):
        return pltpu.make_async_remote_copy(
            src_ref=unit_ref.at[i], dst_ref=recv_ref.at[me, i],
            send_sem=send_sem.at[k, i], recv_sem=recv_sem.at[k, i],
            device_id={"owner": lax.rem(me + 2 * k, n)},
        )

    def forward_copy(k, i):
        source = lax.rem(me + n - 2 * k, n)
        return pltpu.make_async_remote_copy(
            src_ref=recv_ref.at[source, i], dst_ref=recv_ref.at[source, i],
            send_sem=fwd_send.at[k, i], recv_sem=fwd_recv.at[k, i],
            device_id={"owner": sibling},
        )

    side = pltpu.make_async_remote_copy(
        src_ref=unit_ref, dst_ref=recv_ref.at[me],
        send_sem=side_send, recv_sem=side_recv, device_id={"owner": sibling},
    )

    for d in range(1, n):
        list_copy(d).start()
    for k in range(1, chips):
        for i in range(blocks):
            cross_copy(k, i).start()
    side.start()

    every = unit_ref[...].reshape(blocks * BLOCK, width)

    @pl.loop(0, blocks // 2)
    def _(c):
        rows = unit_ref[pl.ds(2 * c, 2)].reshape(2 * BLOCK, width)
        upper = jnp.broadcast_to(mask_ref[2 * c], (BLOCK, blocks * BLOCK))
        lower = jnp.broadcast_to(mask_ref[2 * c + 1], (BLOCK, blocks * BLOCK))
        weights = kernel_of(rows, every) * jnp.concatenate([upper, lower], axis=0)
        total = jnp.sum(weights, axis=1, keepdims=True)
        dens_ref[pl.ds(2 * c, 2)] = jnp.broadcast_to(total, (2 * BLOCK, LANES)).reshape(2, BLOCK, LANES)
        near = jnp.dot(weights.astype(jnp.bfloat16), every, preferred_element_type=jnp.float32)
        acc_ref[pl.ds(2 * c, 2)] = near.reshape(2, BLOCK, width)

    for i in range(blocks):
        for k in range(1, chips):
            cross_copy(k, i).wait_recv()
            forward_copy(k, i).start()
    side.wait()
    for d in range(1, n):
        list_copy(d).wait()
    for i in range(blocks):
        for k in range(1, chips):
            cross_copy(k, i).wait_send()
            forward_copy(k, i).wait()


def far_kernel(
    n, shifts, rows, lists_ref, all_lists_ref, unit_ref, acc_in, dens_in, recv_ref,
    out_ref, log_ref, acc_ref, dens_ref, near_ids, far_ids, held, sems, copy_sem,
):
    me = lax.axis_index("owner")
    blocks = unit_ref.shape[0]
    width = unit_ref.shape[2]

    def add(total, near, far):
        near_ids[total] = near
        far_ids[total] = far

    total = jnp.int32(0)
    for s in range(1, shifts):
        ahead = lax.rem(me + s, n)
        behind = lax.rem(me + n - s, n)
        count = lists_ref[shifts + s, 0]

        @pl.loop(0, count)
        def _(t, total=total, ahead=ahead, s=s):
            add(total + t, lists_ref[s, 2 * t], ahead * blocks + lists_ref[s, 2 * t + 1])

        total = total + count
        count = all_lists_ref[behind * rows + shifts + s, 0]

        @pl.loop(0, count)
        def _(t, total=total, behind=behind, s=s):
            row = behind * rows + s
            add(total + t, all_lists_ref[row, 2 * t + 1], behind * blocks + all_lists_ref[row, 2 * t])

        total = total + count

    def fetch(t):
        return pltpu.make_async_copy(recv_ref.at[far_ids[t]], held.at[lax.rem(t, 2)], sems.at[lax.rem(t, 2)])

    @pl.when(total > 0)
    def _():
        fetch(0).start()

    acc_ref[...] = acc_in[...]
    dens_ref[...] = dens_in[...]

    @pl.loop(0, total)
    def _(t):
        @pl.when(t + 1 < total)
        def _():
            fetch(t + 1).start()

        fetch(t).wait()
        a = near_ids[t]
        other = held[lax.rem(t, 2)]
        weights = kernel_of(unit_ref[a], other)
        dens_ref[a] += jnp.broadcast_to(jnp.sum(weights, axis=1, keepdims=True), (BLOCK, LANES))
        acc_ref[a] += jnp.dot(weights.astype(jnp.bfloat16), other, preferred_element_type=jnp.float32)

    @pl.loop(0, blocks)
    def _(i):
        dens = dens_ref[i]
        share = acc_ref[i] / dens[:, 0:1]
        out_ref[i] = (unit_ref[i].astype(jnp.float32) - share).astype(jnp.bfloat16)
        log_ref[i] = jnp.log(dens.T[0:1])


def shards(embeddings, home_pairs, home_count, surplus_pairs):
    n = lax.axis_size("owner")
    width = embeddings.shape[1]
    blocks = embeddings.shape[0] // BLOCK
    shifts = home_pairs.shape[2]
    slots = home_pairs.shape[3]
    surplus = surplus_pairs.shape[2]
    lanes = 2 * slots
    rows = -(-(2 * shifts + 1) // 8) * 8

    extra = surplus_pairs[0, 0].reshape(1, -1)
    lists = jnp.concatenate(
        [
            home_pairs[0, 0].reshape(shifts, lanes),
            jnp.broadcast_to(home_count[0, 0][:, None], (shifts, lanes)),
            jnp.pad(extra, ((0, rows - 2 * shifts - 1), (0, lanes - extra.shape[1]))),
        ],
        axis=0,
    )
    emb = embeddings.reshape(blocks, BLOCK, width)
    vmem = pl.BlockSpec(memory_space=VMEM)
    smem = pl.BlockSpec(memory_space=SMEM)
    anyw = pl.BlockSpec(memory_space=ANY)
    shape = jax.ShapeDtypeStruct

    unit, mask = pl.pallas_call(
        functools.partial(prep_kernel, shifts, surplus),
        out_shape=(
            shape((blocks, BLOCK, width), jnp.bfloat16),
            shape((blocks, 1, blocks * BLOCK), jnp.float32),
        ),
        in_specs=[smem, vmem],
        out_specs=(vmem, vmem),
        compiler_params=pltpu.CompilerParams(vmem_limit_bytes=VMEM_BYTES),
    )(lists, emb)

    chips = n // 2
    dma = pltpu.SemaphoreType.DMA
    recv, all_lists, acc, dens = pl.pallas_call(
        functools.partial(exchange_kernel, n),
        out_shape=(
            shape((n, blocks, BLOCK, width), jnp.bfloat16),
            shape((n, rows, lanes), jnp.int32),
            shape((blocks, BLOCK, width), jnp.float32),
            shape((blocks, BLOCK, LANES), jnp.float32),
        ),
        in_specs=[vmem, anyw, vmem],
        out_specs=(anyw, anyw, vmem, vmem),
        scratch_shapes=[
            dma((chips, blocks)), dma((chips, blocks)), dma, dma,
            dma((chips, blocks)), dma((chips, blocks)), dma((n,)), dma((n,)),
        ],
        compiler_params=pltpu.CompilerParams(
            collective_id=0, has_side_effects=True, vmem_limit_bytes=VMEM_BYTES
        ),
    )(unit, lists, mask)

    entries = 2 * shifts * slots
    centered, log_density = pl.pallas_call(
        functools.partial(far_kernel, n, shifts, rows),
        out_shape=(
            shape((blocks, BLOCK, width), jnp.bfloat16),
            shape((blocks, 1, BLOCK), jnp.float32),
        ),
        in_specs=[smem, smem, vmem, vmem, vmem, anyw],
        out_specs=(vmem, vmem),
        scratch_shapes=[
            pltpu.VMEM((blocks, BLOCK, width), jnp.float32),
            pltpu.VMEM((blocks, BLOCK, LANES), jnp.float32),
            pltpu.SMEM((entries,), jnp.int32),
            pltpu.SMEM((entries,), jnp.int32),
            pltpu.VMEM((2, BLOCK, width), jnp.bfloat16),
            dma((2,)),
            dma,
        ],
        compiler_params=pltpu.CompilerParams(vmem_limit_bytes=VMEM_BYTES),
    )(lists, all_lists.reshape(n * rows, lanes), unit, acc, dens, recv.reshape(n * blocks, BLOCK, width))
    return (centered.reshape(-1, width), log_density.reshape(-1))


def solution(mesh):
    return jax.shard_map(
        shards,
        mesh=mesh,
        in_specs=(
            P(("group", "owner"), None),
            P("group", "owner", None, None, None),
            P("group", "owner", None),
            P("group", "owner", None, None),
        ),
        out_specs=(P(("group", "owner"), None), P(("group", "owner"))),
        check_vma=False,
    )
```

profile of v0, /device:TPU:19, one launch (start us, length us, event | category | flops | bytes accessed | tf_op | source)
XLA Modules:
  0.0 73.5 jit_solution(14727150792987030334)
XLA Ops:
  0.6 0.7 pad.6.clone
  1.4 0.8 %copy.9 = s32[1,1,8,3]{3,2,1,0:T(8,128)S(1)} copy(s32[1,1,8,3]{2,1,3,0:T(1,128)} %param.7) | data formatting | bytes 192 | tf_op args[3]
  2.1 0.1 reshape_squeeze.7
  2.2 0.8 %copy.8 = s32[1,1,3,64,2]{4,3,2,1,0:T(8,128)S(1)} copy(s32[1,1,3,64,2]{3,4,2,1,0:T(2,128)} %param.5) | data formatting | bytes 3072 | tf_op args[1]
  3.0 0.1 reshape_squeeze.6
  3.1 0.7 pad_add_fusion.lists_ref
  3.8 4.3 %shard_map.59 = (bf16[8,128,1024]{2,1,0:T(8,128)(2,1)}, f32[8,1,1024]{2,1,0:T(1,128)}) custom-call(s32[8,128]{1,0:T(8,128)} %pad_add_fusion.lists_ref, bf16[8,128,1024]{2,1,0:T(8,128)(2,1)} %bitcast.11), custom_call_target="tpu_custom_call" | custom-call | tf_op jit(solution)/shard_map/pallas_call | solution.py:219
  8.1 55.0 %shard_map.60 = (bf16[4,8,128,1024]{3,2,1,0:T(8,128)(2,1)}, s32[4,8,128]{2,1,0:T(8,128)}, f32[8,128,1024]{2,1,0:T(8,128)}, f32[8,128,128]{2,1,0:T(8,128)}) custom-call(bf16[8,128,1024]{2,1,0:T(8,128)(2,1)} %get-tuple-element.10.unit_ref, s32[8,128]{1,0:T(8,128)} %pad_add_fusion.lists_ref, f32[8,1,1024]{2,1,0:T(1,128)} %get-tuple-element.11.mask_ref), custom_call_target="tpu_custom_call" | custom-call | tf_op jit(solution)/shard_map/pallas_call | solution.py:232
  63.1 10.5 %shard_map.61 = (bf16[8,128,1024]{2,1,0:T(8,128)(2,1)}, f32[8,1,128]{2,1,0:T(1,128)}) custom-call(s32[8,128]{1,0:T(8,128)} %pad_add_fusion.lists_ref, s32[32,128]{1,0:T(8,128)} %bitcast.12, bf16[8,128,1024]{2,1,0:T(8,128)(2,1)} %get-tuple-element.10.unit_ref, f32[8,128,1024]{2,1,0:T(8,128)} %get-tuple-element.13.acc_in, ...), custom_call_target="tpu_custom_call" | custom-call | tf_op jit(solution)/shard_map/pallas_call | solution.py:252
where the time goes:
time: 74 us; the launch traced here: 73.5 us
  Pallas kernels  69.7 us (94%)
  local copies, waits for them, and re-layouts  2.5 us (3%)
    pallas_call x1, Pallas kernels, shards(): pl.pallas_call(functools.partial(exchange_kernel, n), out_shape=(shape((n...  55 us
    pallas_call x1, Pallas kernels, shards(): pl.pallas_call(functools.partial(far_kernel, n, shifts, rows), out_shape=...  10.5 us
    pallas_call x1, Pallas kernels, shards(): pl.pallas_call(functools.partial(prep_kernel, shifts, surplus), out_shape...  4.29 us
    unnamed x2, local copies, waits for them, and re-layouts  1.55 us

commit v1 on v0

v1 whole, which is shorter than its diff:
```python
import functools

import jax
import jax.numpy as jnp
from jax import lax
from jax.experimental import pallas as pl
from jax.experimental.pallas import tpu as pltpu
from jax.sharding import PartitionSpec as P

BLOCK = 128
LANES = 128
FIRST = 5
EXTRA = (1, 2, 4)
RING = 8

sharpness = 4.0
epsilon = 1e-06

VMEM = pltpu.MemorySpace.VMEM
SMEM = pltpu.MemorySpace.SMEM
ANY = pl.ANY
F32 = jnp.float32
BF16 = jnp.bfloat16
I32 = jnp.int32


def kernel_of(first, second):
    width = first.shape[-1]
    similarity = lax.dot_general(first, second, (((1,), (1,)), ((), ())), preferred_element_type=F32)
    return jnp.exp(similarity * (sharpness / width) - sharpness)


def iota(shape, axis):
    return lax.broadcasted_iota(I32, shape, axis)


def flag(value):
    return jnp.where(value, 1.0, 0.0).astype(BF16)


def over_lanes(left, right):
    return lax.dot_general(
        left.astype(BF16), right.astype(BF16), (((1,), (1,)), ((), ())), preferred_element_type=F32
    )


def across(left, right):
    return jnp.dot(left.astype(BF16), right.astype(BF16), preferred_element_type=F32)


def adjacency(shifts, blocks, pairs_ref, count_ref, surplus_ref):
    slots = pairs_ref.shape[2]
    tile = jnp.zeros((blocks, LANES), F32)
    for s in range(shifts):
        live = iota((blocks, slots), 1) < count_ref[0:1, s : s + 1]
        left = flag(live & (iota((blocks, slots), 0) == pairs_ref[s, 0:1, :]))
        right = flag(iota((LANES, slots), 0) == pairs_ref[s, 1:2, :] + blocks * s)
        tile = tile + over_lanes(left, right)
    rows, lanes = iota((blocks, LANES), 0), iota((blocks, LANES), 1)
    for t in range(surplus_ref.shape[3]):
        first = surplus_ref[0, 0, :, t : t + 1]
        second = surplus_ref[0, 1, :, t : t + 1]
        live = surplus_ref[0, 2, :, t : t + 1] == 1
        tile = tile + jnp.where((rows == first) & (lanes == second) & live, 1.0, 0.0)
    return tile


def slot_plan(n, shifts, blocks, tiles_ref, every):
    lanes = iota((blocks, LANES), 1)
    rows = iota((blocks, LANES), 0)
    apart = lanes // blocks
    listed = over_lanes(
        jnp.where((apart >= 2 - rows) & (apart < shifts) & (rows < 2), 1.0, 0.0), every
    )
    need = jnp.where((lanes // blocks) % 2 == 0, listed[0:1], listed[1:2])
    named = jnp.zeros((blocks, LANES), F32)
    for q in range(n):
        column = jnp.sum(tiles_ref[q], axis=0, keepdims=True)
        column = jnp.where((apart >= 2 - q % 2) & (apart < shifts), column, 0.0)
        named = named + (pltpu.roll(column, blocks * q, 1) if q else column)
    named = named + pltpu.roll(named, LANES - blocks * n, 1)
    need = jnp.where((need + named > 0.0) & (lanes < blocks * n), 1.0, 0.0)
    left, right = iota((LANES, LANES), 0), iota((LANES, LANES), 1)
    same = left // (2 * blocks) == right // (2 * blocks)
    place = across(need, flag(same & (left < right)))
    total = across(need, flag(same))
    most = jnp.max(total, axis=1, keepdims=True)
    return need, place, most


def work_list(n, shifts, blocks, me, mine, every, place):
    chips = n // 2
    left, right = iota((LANES, LANES), 0), iota((LANES, LANES), 1)
    apart = left // blocks
    ahead = apart + me
    ahead = jnp.where(ahead >= n, ahead - n, ahead)
    move = flag((apart >= 1) & (apart < shifts) & (right == ahead * blocks + left % blocks))
    far = across(mine, move)
    turned = over_lanes(flag(left == right), every)
    lanes = iota((blocks, LANES), 1)
    owner = lanes // blocks
    behind = me - owner
    behind = jnp.where(behind < 0, behind + n, behind)
    for s in range(1, shifts):
        far = far + jnp.where((behind == s) & (owner < n), turned[s * blocks : (s + 1) * blocks], 0.0)
    step = owner // 2 - me // 2
    step = jnp.where(step < 0, step + chips, step).astype(F32)
    code = jnp.where(
        step == 0.0, (lanes % blocks).astype(F32), blocks + (step - 1.0) * (2 * blocks) + place
    )
    order = across(jnp.where(far > 0.0, 1.0, 0.0), flag(left < right))
    rest = jnp.where(far > 0.0, order, -1.0)
    work = jnp.zeros((blocks, LANES), F32)
    for j in range(blocks + (chips - 1) * 2 * blocks):
        value = jnp.sum(jnp.where(rest == float(j), code, 0.0), axis=1, keepdims=True)
        work = jnp.where(lanes == j, value, work)
    number = jnp.sum(jnp.where(far > 0.0, 1.0, 0.0), axis=1, keepdims=True)
    return jnp.where(lanes == LANES - 1, number, work).astype(I32)


def front_kernel(
    n, groups, shifts, limits, pairs_ref, count_ref, surplus_ref, emb_ref,
    chip_out, acc_out, dens_ref, pack_out, recv_ref, work_ref, level_ref,
    emb, chip, acc, pack, tiles, mask, maxima, found,
    emb_sem, push_send, push_recv, list_send, list_recv, slot_send, slot_recv,
    fwd_send, fwd_recv, max_send, max_recv, chip_sem, pack_sem, acc_sem,
):
    me = lax.axis_index("owner")
    group = lax.axis_index("group")
    blocks, _, width = emb_ref.shape
    chips = n // 2
    half = BLOCK // 2
    core = lax.rem(me, 2)
    sibling = me + 1 - 2 * core
    steps = groups.bit_length() - 1
    upper = pl.multiple_of(core * half, half)

    def partner(k):
        bit = lax.rem(group // (1 << k), 2)
        return group + (1 << k) * (1 - 2 * bit)

    barrier = pltpu.get_barrier_semaphore()
    for d in range(1, n):
        pl.semaphore_signal(barrier, inc=1, device_id={"owner": lax.rem(me + d, n)})
    for k in range(steps):
        pl.semaphore_signal(barrier, inc=1, device_id={"group": partner(k)})

    def fetch(i):
        return pltpu.make_async_copy(emb_ref.at[i], emb.at[i], emb_sem.at[i])

    def push(i):
        return pltpu.make_async_remote_copy(
            src_ref=chip.at[core * blocks + i], dst_ref=chip.at[core * blocks + i],
            send_sem=push_send.at[i], recv_sem=push_recv.at[i], device_id={"owner": sibling},
        )

    def keep(i):
        return pltpu.make_async_copy(chip.at[i], chip_out.at[i], chip_sem.at[i])

    def list_copy(d):
        return pltpu.make_async_remote_copy(
            src_ref=tiles.at[me], dst_ref=tiles.at[me],
            send_sem=list_send.at[d], recv_sem=list_recv.at[d],
            device_id={"owner": lax.rem(me + d, n)},
        )

    def slot_copy(k, j):
        return pltpu.make_async_remote_copy(
            src_ref=pack.at[j], dst_ref=recv_ref.at[chips - k - 1, j, pl.ds(upper, half)],
            send_sem=slot_send.at[k, j], recv_sem=slot_recv.at[k, j],
            device_id={"owner": lax.rem(me + 2 * k, n)},
        )

    def forward(k, j):
        return pltpu.make_async_remote_copy(
            src_ref=recv_ref.at[chips - k - 1, j, pl.ds(upper, half)],
            dst_ref=recv_ref.at[chips - k - 1, j, pl.ds(upper, half)],
            send_sem=fwd_send.at[k, j], recv_sem=fwd_recv.at[k, j], device_id={"owner": sibling},
        )

    def max_copy(k):
        return pltpu.make_async_remote_copy(
            src_ref=maxima.at[k], dst_ref=found.at[k],
            send_sem=max_send.at[k], recv_sem=max_recv.at[k], device_id={"group": partner(k)},
        )

    def save(c):
        return pltpu.make_async_copy(acc.at[pl.ds(2 * c, 2)], acc_out.at[pl.ds(2 * c, 2)], acc_sem.at[c])

    @pl.loop(0, blocks)
    def _(i):
        fetch(i).start()

    mine = adjacency(shifts, blocks, pairs_ref, count_ref, surplus_ref)
    for q in range(n, LANES // blocks):
        tiles[q] = jnp.zeros((blocks, LANES), F32)
    tiles[me] = mine

    lanes = iota((blocks, LANES), 1)
    turned = over_lanes(flag(lanes == iota((blocks, LANES), 0)), mine)
    near = jnp.where(mine[:, 0:blocks] + turned > 0.0, 1.0, 0.0)
    wide = jnp.concatenate(
        [jnp.broadcast_to(near[:, b : b + 1], (blocks, BLOCK)) for b in range(blocks)], axis=1
    )
    for a in range(blocks):
        mask[a] = wide[a : a + 1]

    def normalize(i):
        fetch(i).wait()
        values = emb[i].astype(F32)
        inv = lax.rsqrt(jnp.mean(values * values, axis=-1, keepdims=True) + epsilon)
        chip[core * blocks + i] = (values * inv).astype(BF16)

    pl.semaphore_wait(barrier, n - 1 + steps)
    for d in range(1, n):
        list_copy(d).start()

    @pl.loop(0, blocks)
    def _(i):
        normalize(i)
        push(i).start()

    for d in range(1, n):
        list_copy(d).wait_recv()
    every = tiles[...].reshape(LANES, LANES)
    need, place, most = slot_plan(n, shifts, blocks, tiles, every)
    maxima[0] = jnp.broadcast_to(most, (blocks, LANES))
    max_copy(0).start()

    here = (need > 0.0) & (lanes // (2 * blocks) == me // 2)
    rank = jnp.where(here, place, -1.0)[0:1]
    spot = (lanes % (2 * blocks)).astype(F32)[0:1]

    for i in range(blocks):
        push(i).wait_recv()

    for j in range(2 * blocks):
        index = jnp.clip(jnp.sum(jnp.where(rank == float(j), spot, 0.0)).astype(I32), 0, 2 * blocks - 1)
        pack[j] = chip[index, pl.ds(upper, half), :]
        if j < limits[0]:
            for k in range(1, chips):
                slot_copy(k, j).start()

    @pl.loop(0, 2 * blocks)
    def _(i):
        keep(i).start()

    save_pack = pltpu.make_async_copy(pack, pack_out, pack_sem)
    save_pack.start()
    work_ref[...] = work_list(n, shifts, blocks, me, mine, every, place)

    own = chip.at[pl.ds(core * blocks, blocks)]

    @pl.loop(0, blocks // 2)
    def _(c):
        full = own[...].reshape(blocks * BLOCK, width)
        rows = own[pl.ds(2 * c, 2)].reshape(2 * BLOCK, width)
        first = jnp.broadcast_to(mask[2 * c], (BLOCK, blocks * BLOCK))
        second = jnp.broadcast_to(mask[2 * c + 1], (BLOCK, blocks * BLOCK))
        weights = kernel_of(rows, full) * jnp.concatenate([first, second], axis=0)
        total = jnp.sum(weights, axis=1, keepdims=True)
        dens_ref[pl.ds(2 * c, 2)] = jnp.broadcast_to(total, (2 * BLOCK, LANES)).reshape(2, BLOCK, LANES)
        close = jnp.dot(weights.astype(BF16), full, preferred_element_type=F32)
        acc[pl.ds(2 * c, 2)] = close.astype(BF16).reshape(2, BLOCK, width)
        save(c).start()

    for k in range(steps):
        max_copy(k).wait_recv()
        maxima[k + 1] = jnp.maximum(maxima[k], found[k])
        if k + 1 < steps:
            max_copy(k + 1).start()
    most = maxima[steps]
    level = jnp.zeros_like(most)
    for limit in limits:
        level = level + jnp.where(most > float(limit), 1.0, 0.0)
    level_ref[0] = jnp.max(level).astype(I32)

    for j in range(limits[0]):
        for k in range(1, chips):
            slot_copy(k, j).wait_recv()
            forward(k, j).start()
    for i in range(blocks):
        push(i).wait_send()
    for d in range(1, n):
        list_copy(d).wait_send()
    for k in range(steps):
        max_copy(k).wait_send()
    for i in range(2 * blocks):
        keep(i).wait()
    save_pack.wait()
    for c in range(blocks // 2):
        save(c).wait()
    for j in range(limits[0]):
        for k in range(1, chips):
            slot_copy(k, j).wait_send()
            forward(k, j).wait()


def more_kernel(n, base, count, pack_ref, recv_ref, slot_send, slot_recv, fwd_send, fwd_recv):
    me = lax.axis_index("owner")
    chips = n // 2
    half = BLOCK // 2
    core = lax.rem(me, 2)
    sibling = me + 1 - 2 * core
    upper = pl.multiple_of(core * half, half)

    barrier = pltpu.get_barrier_semaphore()
    for d in range(1, n):
        pl.semaphore_signal(barrier, inc=1, device_id={"owner": lax.rem(me + d, n)})
    pl.semaphore_wait(barrier, n - 1)

    def slot_copy(k, j):
        return pltpu.make_async_remote_copy(
            src_ref=pack_ref.at[base + j], dst_ref=recv_ref.at[chips - k - 1, j, pl.ds(upper, half)],
            send_sem=slot_send.at[k, j], recv_sem=slot_recv.at[k, j],
            device_id={"owner": lax.rem(me + 2 * k, n)},
        )

    def forward(k, j):
        return pltpu.make_async_remote_copy(
            src_ref=recv_ref.at[chips - k - 1, j, pl.ds(upper, half)],
            dst_ref=recv_ref.at[chips - k - 1, j, pl.ds(upper, half)],
            send_sem=fwd_send.at[k, j], recv_sem=fwd_recv.at[k, j], device_id={"owner": sibling},
        )

    for j in range(count):
        for k in range(1, chips):
            slot_copy(k, j).start()
    for j in range(count):
        for k in range(1, chips):
            slot_copy(k, j).wait_recv()
            forward(k, j).start()
    for j in range(count):
        for k in range(1, chips):
            slot_copy(k, j).wait_send()
            forward(k, j).wait()


def finish_kernel(n, base, work_ref, chip_ref, acc_ref, dens_ref, *refs):
    recvs = refs[: 2 if base else 1]
    (out_ref, log_ref, unit, acc, dens, near, out, held, codes,
     unit_sem, acc_sem, dens_sem, held_sem, out_sem) = refs[len(recvs):]
    me = lax.axis_index("owner")
    core = lax.rem(me, 2)
    blocks = unit.shape[0]
    first = recvs[0].shape[1]

    def load(i):
        return (
            pltpu.make_async_copy(chip_ref.at[core * blocks + i], unit.at[i], unit_sem.at[i]),
            pltpu.make_async_copy(acc_ref.at[i], acc.at[i], acc_sem.at[i]),
            pltpu.make_async_copy(dens_ref.at[i], dens.at[i], dens_sem.at[i]),
        )

    def store(i):
        return pltpu.make_async_copy(out.at[i], out_ref.at[i], out_sem.at[i])

    @pl.loop(0, blocks)
    def _(i):
        for copy in load(i):
            copy.start()

    def slot(t):
        return held.at[lax.rem(t, RING)], held_sem.at[lax.rem(t, RING)]

    def fetch(t):
        code = codes[t]
        place, sem = slot(t)

        @pl.when(code < blocks)
        def _():
            pltpu.make_async_copy(chip_ref.at[(1 - core) * blocks + code], place, sem).start()

        other = jnp.maximum(code - blocks, 0)
        chip, spot = other // (2 * blocks), lax.rem(other, 2 * blocks)

        @pl.when((code >= blocks) & (spot < first))
        def _():
            pltpu.make_async_copy(recvs[0].at[chip, jnp.minimum(spot, first - 1)], place, sem).start()

        if base:
            @pl.when((code >= blocks) & (spot >= first))
            def _():
                pltpu.make_async_copy(recvs[1].at[chip, jnp.maximum(spot - first, 0)], place, sem).start()

    total = jnp.int32(0)
    starts = []
    for a in range(blocks):
        number = work_ref[a, LANES - 1]
        starts.append(total)

        @pl.loop(0, number)
        def _(t, total=total, a=a):
            codes[total + t] = work_ref[a, t]

        total = total + number
    starts.append(total)

    @pl.loop(0, jnp.minimum(total, RING))
    def _(t):
        fetch(t)

    for i in range(blocks):
        for copy in load(i):
            copy.wait()

        near[...] = acc[i].astype(F32)

        @pl.loop(starts[i], starts[i + 1])
        def _(t):
            place, sem = slot(t)
            pltpu.make_async_copy(chip_ref.at[0], place, sem).wait()
            other = place[...]
            weights = kernel_of(unit[i], other)
            dens[i] += jnp.broadcast_to(jnp.sum(weights, axis=1, keepdims=True), (BLOCK, LANES))
            near[...] += jnp.dot(weights.astype(BF16), other, preferred_element_type=F32)

            @pl.when(t + RING < total)
            def _():
                fetch(t + RING)

        density = dens[i]
        share = near[...] * (1.0 / density[:, 0:1])
        out[i] = (unit[i].astype(F32) - share).astype(BF16)
        log_ref[i] = jnp.log(density.T[0:1])
        store(i).start()

    for i in range(blocks):
        store(i).wait()


def shards(groups, embeddings, home_pairs, home_count, surplus_pairs):
    n = lax.axis_size("owner")
    chips = n // 2
    width = embeddings.shape[1]
    blocks = embeddings.shape[0] // BLOCK
    shifts, slots = home_pairs.shape[2], home_pairs.shape[3]
    most = 2 * blocks
    extra = tuple(e for e in EXTRA if FIRST + e < most) + (most - FIRST,)
    limits = (FIRST,) + tuple(FIRST + e for e in extra[:-1])

    pairs = home_pairs[0, 0].transpose(0, 2, 1)
    count = home_count[0, 0].reshape(1, shifts)
    chosen = surplus_pairs.transpose(0, 3, 1, 2)
    emb = embeddings.reshape(blocks, BLOCK, width)
    vmem = pl.BlockSpec(memory_space=VMEM)
    smem = pl.BlockSpec(memory_space=SMEM)
    anyw = pl.BlockSpec(memory_space=ANY)
    shape = jax.ShapeDtypeStruct
    dma = pltpu.SemaphoreType.DMA
    half = BLOCK // 2
    steps = groups.bit_length() - 1

    chip, acc, dens, pack, recv, work, level = pl.pallas_call(
        functools.partial(front_kernel, n, groups, shifts, limits),
        out_shape=(
            shape((2 * blocks, BLOCK, width), BF16),
            shape((blocks, BLOCK, width), BF16),
            shape((blocks, BLOCK, LANES), F32),
            shape((2 * blocks, half, width), BF16),
            shape((chips - 1, FIRST, BLOCK, width), BF16),
            shape((blocks, LANES), I32),
            shape((1,), I32),
        ),
        in_specs=[vmem, vmem, vmem, anyw],
        out_specs=(anyw, anyw, vmem, anyw, anyw, vmem, smem),
        scratch_shapes=[
            pltpu.VMEM((blocks, BLOCK, width), BF16),
            pltpu.VMEM((2 * blocks, BLOCK, width), BF16),
            pltpu.VMEM((blocks, BLOCK, width), BF16),
            pltpu.VMEM((2 * blocks, half, width), BF16),
            pltpu.VMEM((LANES // blocks, blocks, LANES), F32),
            pltpu.VMEM((blocks, 1, blocks * BLOCK), F32),
            pltpu.VMEM((steps + 1, blocks, LANES), F32),
            pltpu.VMEM((steps, blocks, LANES), F32),
            dma((blocks,)), dma((blocks,)), dma((blocks,)), dma((n,)), dma((n,)),
            dma((chips, FIRST)), dma((chips, FIRST)), dma((chips, FIRST)), dma((chips, FIRST)),
            dma((steps,)), dma((steps,)), dma((2 * blocks,)), dma, dma((blocks // 2,)),
        ],
        compiler_params=pltpu.CompilerParams(
            collective_id=0, has_side_effects=True, vmem_limit_bytes=56 * 1024 * 1024
        ),
    )(pairs, count, chosen, emb)

    def finish(base, recvs, work, chip, acc, dens):
        entries = blocks * (LANES - 1)
        return pl.pallas_call(
            functools.partial(finish_kernel, n, base),
            out_shape=(
                shape((blocks, BLOCK, width), BF16),
                shape((blocks, 1, BLOCK), F32),
            ),
            in_specs=[smem] + [anyw] * (3 + len(recvs)),
            out_specs=(anyw, vmem),
            scratch_shapes=[
                pltpu.VMEM((blocks, BLOCK, width), BF16),
                pltpu.VMEM((blocks, BLOCK, width), BF16),
                pltpu.VMEM((blocks, BLOCK, LANES), F32),
                pltpu.VMEM((BLOCK, width), F32),
                pltpu.VMEM((blocks, BLOCK, width), BF16),
                pltpu.VMEM((RING, BLOCK, width), BF16),
                pltpu.SMEM((entries,), I32),
                dma((blocks,)), dma((blocks,)), dma((blocks,)), dma((RING,)), dma((blocks,)),
            ],
            compiler_params=pltpu.CompilerParams(vmem_limit_bytes=56 * 1024 * 1024),
        )(work, chip, acc, dens, *recvs)

    def enough(work, chip, acc, dens, pack, recv):
        return finish(0, (recv,), work, chip, acc, dens)

    def with_more(rank, number, work, chip, acc, dens, pack, recv):
        later = pl.pallas_call(
            functools.partial(more_kernel, n, FIRST, number),
            out_shape=shape((chips - 1, number, BLOCK, width), BF16),
            in_specs=[anyw],
            out_specs=anyw,
            scratch_shapes=[dma((chips, number)) for _ in range(4)],
            compiler_params=pltpu.CompilerParams(collective_id=1 + rank, has_side_effects=True),
        )(pack)
        return finish(FIRST, (recv, later), work, chip, acc, dens)

    branches = [enough] + [functools.partial(with_more, rank, e) for rank, e in enumerate(extra)]
    centered, log_density = lax.switch(level[0], branches, work, chip, acc, dens, pack, recv)
    return (centered.reshape(-1, width), log_density.reshape(-1))


def solution(mesh):
    return jax.shard_map(
        functools.partial(shards, mesh.shape["group"]),
        mesh=mesh,
        in_specs=(
            P(("group", "owner"), None),
            P("group", "owner", None, None, None),
            P("group", "owner", None),
            P("group", "owner", None, None),
        ),
        out_specs=(P(("group", "owner"), None), P(("group", "owner"))),
        check_vma=False,
    )
```

time: 74 us -> 35.6 us (0.48)
  the two profiles are of different devices: /device:TPU:19 before, /device:TPU:0 now
where the time goes in v1:
time: 35.6 us; the launch traced here: 35.1 us
  Pallas kernels  33.4 us (94%)
  between operations  1.5 us (4%)
    pallas_call x1, Pallas kernels, shards(): pl.pallas_call(functools.partial(front_kernel, n, groups, shifts, limits)...  27.8 us
    pallas_call x1, Pallas kernels, finish(): pl.pallas_call(functools.partial(finish_kernel, n, base), out_shape=(shap...  5.56 us

profile of v1, /device:TPU:0, one launch (start us, length us, event | category | flops | bytes accessed | tf_op | source)
XLA Modules:
  0.0 35.1 jit_solution(13706269376983179320)
XLA Ops:
  0.6 27.8 %shard_map.59 = (bf16[16,128,1024]{2,1,0:T(8,128)(2,1)}, bf16[8,128,1024]{2,1,0:T(8,128)(2,1)S(1)}, f32[8,128,128]{2,1,0:T(8,128)}, bf16[16,64,1024]{2,1,0:T(8,1...) custom-call(s32[3,2,64]{2,1,0:T(2,128)} %bitcast.10, s32[1,3]{1,0:T(1,128)} %bitcast.12, ...), custom_call_target="tpu_custom_call" | custom-call | tf_op jit(solution)/shard_map/pallas_call | solution.py:454
  29.1 5.8 %conditional.1 = ((bf16[8,128,1024]{2,1,0:T(8,128)(2,1)}, f32[8,1,128]{2,1,0:T(1,128)})) conditional(s32[]{:T(128)} %bitcast.5, (s32[8,128]{1,0:T(8,128)S(1)}, bf16[16,128,1024]{2,1,0:T(8,128)(2,1)}, bf16[8,128,1024]{2,1,0:T(8,128)(2,1)S(1)}, f32[8,128,128]{2,1,0:T(8,128)}, ...), branch_computations={%region_0.0_spmd, %region_1.0_spmd, %region_2.0_spmd, %region_3.0_... | conditional | bytes 8 | solution.py:523
  29.1 5.6 %branch_0_fun.1 = (bf16[8,128,1024]{2,1,0:T(8,128)(2,1)}, f32[8,1,128]{2,1,0:T(1,128)}) custom-call(s32[8,128]{1,0:T(8,128)S(1)} %get-tuple-element.70.work_ref, bf16[16,128,1024]{2,1,0:T(8,128)(2,1)} %get-tuple-element.71.chip_ref, bf16[8,128,1024]{2,1,0:T(8,128)(2,1)S(1)} %get-tuple-element.72.acc_ref, f32[8,128,128]{2,1,0:T(8,128)} %get-tuple-element.73.dens_ref, ...), custom_call_target="tpu_custom_call" | custom-call | tf_op jit(solution)/shard_map/cond/branch_0_fun/pallas_call | solution.py:487
